TPU v7x, 512 devices: a whole 4x8x8 slice. The times are simulated.
512 devices in a mesh: dp: 4 (over x), expert: 16 (over z, core), etp: 8 (over y).
Axes of the slice: x: 4, y: 8, z: 8, core: 2. Of those that a mesh axis runs over, the one named last changes fastest.
Arguments:
- tokens: bfloat16 [9728, 4096], P(('dp', 'expert'), 'etp'), may hold values from -6 to 6
- cotangent: bfloat16 [9728, 4096], P(('dp', 'expert'), 'etp'), may hold values from -6 to 6
- gates: bfloat16 [9728, 8], P(('dp', 'expert')), may hold values from 0.049804688 to 0.5
- experts_hit: int32 [9728, 8], P(('dp', 'expert')), may hold values from -1 to 15, as said below
- positions: int32 [9728, 8], P(('dp', 'expert')), may hold values from -1 to 18, as said below
- gate_w: bfloat16 [16, 4096, 1536], P('expert', 'dp', 'etp'), may hold values from -0.09375 to 0.09375
- up_w: bfloat16 [16, 4096, 1536], P('expert', 'dp', 'etp'), may hold values from -0.09375 to 0.09375
- down_w: bfloat16 [16, 1536, 4096], P('expert', 'etp', 'dp'), may hold values from -0.15625 to 0.15625
Outputs:
- input_grad: bfloat16 [9728, 4096], P(('dp', 'expert'), 'etp')
- down_grad: bfloat16 [16, 1536, 4096], P('expert', 'etp', 'dp')
Inputs may be any that keep to these rules, and one draw needn't show every extreme that they name: experts_hit and positions are -1 together, for routes to experts outside these 16. In the rows of one device, the routes to one expert hold positions 0 to n - 1 once each, with n between 1 and 19; no token names an expert twice. `positions`: see experts_hit.
All inputs are finite; a program needn't handle non-finite values.
Results may differ from a plain program's by a relative error of at most 0.018.
Values may be sent and summed in bfloat16 or wider, within the bound.
No kernel may reach another device: no remote copies, remote signals or barrier semaphores. Data moves between devices by JAX's collectives and lax.ppermute only.
A program may use at most 64 MiB of HBM per device.

v0:
```python
import jax
import jax.numpy as jnp
from jax import lax
from jax.sharding import PartitionSpec as P

CAP = 19


def expert_grads(feats, grads, gate_col, w_gate, w_up, w_down):
    gate_pre = jnp.dot(feats, w_gate, preferred_element_type=jnp.float32)
    up_pre = jnp.dot(feats, w_up, preferred_element_type=jnp.float32)
    sig = jax.nn.sigmoid(gate_pre)
    act = gate_pre * sig
    hidden_b = (act * up_pre).astype(jnp.bfloat16)
    back = lax.dot_general(
        grads, w_down, (((1,), (1,)), ((), ())), preferred_element_type=jnp.float32
    )
    gate_f = gate_col.astype(jnp.float32)[:, None]
    d_hidden = gate_f * back
    d_gate_b = (d_hidden * up_pre * sig * (1.0 + gate_pre * (1.0 - sig))).astype(jnp.bfloat16)
    d_up_b = (d_hidden * act).astype(jnp.bfloat16)
    d_part = lax.dot_general(
        d_gate_b, w_gate, (((1,), (1,)), ((), ())), preferred_element_type=jnp.float32
    )
    d_part = d_part + lax.dot_general(
        d_up_b, w_up, (((1,), (1,)), ((), ())), preferred_element_type=jnp.float32
    )
    scaled = (gate_f * grads).astype(jnp.bfloat16)
    term = lax.dot_general(
        hidden_b, scaled, (((0,), (0,)), ((), ())), preferred_element_type=jnp.float32
    )
    return (d_part.astype(jnp.bfloat16), term)


def local(tokens, cotangent, gates, experts_hit, positions, gate_w, up_w, down_w):
    width = lax.axis_size("expert")
    rows_dev = tokens.shape[0]
    routes = experts_hit.shape[1]
    slots = width * CAP
    valid = experts_hit >= 0
    flat = jnp.where(valid, experts_hit * CAP + positions, slots)
    flat_all = flat.reshape(-1)
    token_ids = jnp.repeat(jnp.arange(rows_dev, dtype=jnp.int32), routes)
    owner = jnp.zeros((slots + 1,), jnp.int32).at[flat_all].set(token_ids)[:slots]
    filled = jnp.zeros((slots + 1,), jnp.bool_).at[flat_all].set(True)[:slots]
    slot_gate = jnp.zeros((slots + 1,), jnp.bfloat16).at[flat_all].set(gates.reshape(-1))[:slots]
    slot_gate = slot_gate.reshape(width, CAP)

    def pack(source):
        rows = jnp.where(filled[:, None], source[owner], jnp.zeros((), source.dtype))
        return rows.reshape(width, CAP, source.shape[1])

    full_x, full_dy = (
        lax.all_gather(tokens, "etp", axis=1, tiled=True),
        lax.all_gather(cotangent, "etp", axis=1, tiled=True),
    )
    recv_x, recv_dy, recv_gate = (
        lax.all_to_all(pack(full_x), "expert", split_axis=0, concat_axis=0, tiled=True),
        lax.all_to_all(pack(full_dy), "expert", split_axis=0, concat_axis=0, tiled=True),
        lax.all_to_all(slot_gate, "expert", split_axis=0, concat_axis=0, tiled=True),
    )
    full_width = recv_x.shape[2]
    feats = recv_x.reshape(slots, full_width)
    grads = recv_dy.reshape(slots, full_width)
    w_gate, w_up, w_down = (
        lax.all_gather(gate_w[0], "dp", axis=0, tiled=True),
        lax.all_gather(up_w[0], "dp", axis=0, tiled=True),
        lax.all_gather(down_w[0], "dp", axis=1, tiled=True),
    )
    d_part_b, term = expert_grads(feats, grads, recv_gate.reshape(slots), w_gate, w_up, w_down)
    down_grad = lax.psum_scatter(term.astype(jnp.bfloat16), "dp", scatter_dimension=1, tiled=True)[
        None
    ]
    summed = lax.psum_scatter(
        d_part_b.astype(jnp.float32).astype(jnp.bfloat16), "etp", scatter_dimension=1, tiled=True
    ).astype(jnp.float32)
    returned = lax.all_to_all(
        summed.reshape(width, CAP, summed.shape[1]).astype(jnp.bfloat16),
        "expert",
        split_axis=0,
        concat_axis=0,
        tiled=True,
    ).astype(jnp.float32)
    narrow = returned.shape[2]
    table = jnp.concatenate(
        [returned.reshape(slots, narrow), jnp.zeros((1, narrow), jnp.float32)], axis=0
    )
    total = jnp.zeros((rows_dev, narrow), jnp.float32)
    for route in range(routes):
        total = total + table[flat[:, route]]
    input_grad = total.astype(jnp.bfloat16)
    return (input_grad, down_grad)


def solution(mesh):
    placed = (
        P(("dp", "expert"), "etp"),
        P(("dp", "expert"), "etp"),
        P(("dp", "expert"), None),
        P(("dp", "expert"), None),
        P(("dp", "expert"), None),
        P("expert", "dp", "etp"),
        P("expert", "dp", "etp"),
        P("expert", "etp", "dp"),
    )
    return jax.shard_map(
        local,
        mesh=mesh,
        in_specs=placed,
        out_specs=(P(("dp", "expert"), "etp"), P("expert", "etp", "dp")),
        check_vma=False,
    )
```

profile of v0, /device:TPU:8, one launch (start us, length us, event | category | flops | bytes accessed | tf_op | source)
XLA Modules:
  0.0 373.5 jit_solution(14487152539822425806)
XLA Ops:
  8.0 0.0 all-gather.9.cloned.1.call-start
  8.0 0.7 all-gather.9.cloned.1.call-update
  8.7 0.0 all-gather.11.cloned.1.call-start
  8.8 0.7 all-gather.11.cloned.1.call-update
  9.5 0.7 add_select_fusion
  10.2 0.1 copy.12
  10.3 0.1 reshape.80
  10.4 0.8 copy.13
  11.2 0.1 reshape.171
  11.4 12.6 %scatter_custom_fusion = bf16[305]{0:T(512)(128)(2,1)S(1)} fusion(s32[1216]{0:T(1024)S(1)} %fusion.18, bf16[1216]{0:T(1024)(128)(2,1)S(1)} %reshape.171, bf16[]{:T(256)} %constant.9.clone.1), kind=kCustom, calls=%fused_computation.64 | custom fusion | bytes 612 | tf_op jit(solution)/shard_map/scatter | solution.py:46
  24.0 0.7 all_to_all.20
  24.7 10.4 %all-to-all-start = ((bf16[16,1,19]{2,1,0:T(2,128)(2,1)}), bf16[16,1,19]{2,1,0:T(2,128)(2,1)S(1)}, u32[]{:S(2)}, u32[]{:S(2)}) async-start(bf16[16,1,19]{2,1,0:T(2,128)(2,1)} %all_to_all.20), calls=%async_computation | async-start | bytes 16384 | tf_op jit(solution)/shard_map/all_to_all | solution.py:60
  35.2 0.1 reshape.187
  35.3 11.4 %scatter_custom_fusion.1 = pred[305]{0:T(512)(128)(4,1)S(1)} fusion(s32[1216]{0:T(1024)S(1)} %fusion.18, pred[1216]{0:T(1024)(128)(4,1)S(1)} %broadcast.66, pred[]{:T(512)} %constant.14.clone.1), kind=kCustom, calls=%fused_computation.62 | custom fusion | bytes 306 | tf_op jit(solution)/shard_map/scatter | solution.py:45
  46.7 0.1 broadcast_in_dim.63
  46.8 6.4 %scatter_custom_fusion.2 = s32[305]{0:T(512)S(1)} fusion(s32[1216]{0:T(1024)S(1)} %fusion.18, s32[1216]{0:T(1024)S(1)} %reshape.187, s32[]{:T(128)} %constant.10.clone.1), kind=kCustom, calls=%fused_computation.60 | custom fusion | bytes 1224 | tf_op jit(solution)/shard_map/scatter | solution.py:44
  53.2 3.7 all-gather.9.cloned.1.call-done
  56.9 9.5 %gather_fusion = bf16[304,4096]{1,0:T(8,128)(2,1)} fusion(bf16[152,4096]{1,0:T(8,128)(2,1)} %all-gather.9.cloned.1.call-done, s32[1024]{0:T(1024)S(1)} %pad_clamp_fusion.8), kind=kCustom, calls=%fused_computation | custom fusion | bytes 4981952 | tf_op jit(solution)/shard_map/gather | solution.py:50
  66.4 2.2 gather.35
  68.5 30.9 %all-gather.11.cloned.1.call-done = bf16[152,4096]{1,0:T(8,128)(2,1)} async-done(((bf16[152,512]{1,0:T(8,128)(2,1)}), bf16[152,4096]{1,0:T(8,128)(2,1)}) %all-gather.11.cloned.1.call-update) | async-done | bytes 1245200 | tf_op jit(solution)/shard_map/all_gather | solution.py:54
  99.4 9.5 %gather_fusion.1 = bf16[304,4096]{1,0:T(8,128)(2,1)} fusion(bf16[152,4096]{1,0:T(8,128)(2,1)} %all-gather.11.cloned.1.call-done, s32[1024]{0:T(1024)S(1)} %pad_clamp_fusion.8), kind=kCustom, calls=%fused_computation.1 | custom fusion | bytes 4981952 | tf_op jit(solution)/shard_map/gather | solution.py:50
  108.9 3.4 gather.37
  112.3 5.0 %broadcast_select_fusion.1 = (bf16[16,19,4096]{2,1,0:T(8,128)(2,1)}, bf16[16,19,4096]{2,1,0:T(8,128)(2,1)}) fusion(bf16[16,19,4096]{2,1,0:T(8,128)(2,1)S(1)} %gather.35, pred[16,19]{1,0:T(8,128)(4,1)S(1)} %broadcast_in_dim.63, bf16[16,19,4096]{2,1,0:T(8,128)(2,1)} %gather.37), kind=kLoop, calls=%fused_computation.18 | loop fusion | flops 2490368 | bytes 9961776 | tf_op jit(solution)/shard_map/jit(_where)/select_n | solution.py:50
  117.3 7.5 %all-to-all-start.1 = ((bf16[16,19,4096]{2,1,0:T(8,128)(2,1)}), bf16[16,19,4096]{2,1,0:T(8,128)(2,1)S(1)}, u32[]{:S(2)}, u32[]{:S(2)}) async-start(bf16[16,19,4096]{2,1,0:T(8,128)(2,1)} %get-tuple-element.10), calls=%async_computation.1 | async-start | bytes 6291456 | tf_op jit(solution)/shard_map/all_to_all | solution.py:59
  124.7 0.0 all-gather.17.cloned.1.call-start
  124.8 0.5 all-gather.17.cloned.1.call-update
  125.3 71.2 %all-to-all-done.1 = bf16[16,19,4096]{2,1,0:T(8,128)(2,1)S(1)} async-done(((bf16[16,19,4096]{2,1,0:T(8,128)(2,1)}), bf16[16,19,4096]{2,1,0:T(8,128)(2,1)S(1)}, u32[]{:S(2)}, u32[]{:S(2)}) %all-to-all-start.1) | async-done | bytes 2490400 | tf_op jit(solution)/shard_map/all_to_all | solution.py:59
  196.5 4.7 %all-to-all-start.2 = ((bf16[16,19,4096]{2,1,0:T(8,128)(2,1)}), bf16[16,19,4096]{2,1,0:T(8,128)(2,1)}, u32[]{:S(2)}, u32[]{:S(2)}) async-start(bf16[16,19,4096]{2,1,0:T(8,128)(2,1)} %get-tuple-element.11), calls=%async_computation.2 | async-start | bytes 6291456 | tf_op jit(solution)/shard_map/all_to_all | solution.py:58
  201.2 0.0 all-gather.15.cloned.1.call-start
  201.3 0.5 all-gather.15.cloned.1.call-update
  201.8 0.0 all-gather.13.cloned.1.call-start
  201.9 0.5 all-gather.13.cloned.1.call-update
  202.4 0.3 reduce-scatter.3.cloned.1.call-start
  202.7 0.1 reshape.86
  202.8 2.1 reshape.83
  204.8 68.2 %all-to-all-done.2 = bf16[16,19,4096]{2,1,0:T(8,128)(2,1)} async-done(((bf16[16,19,4096]{2,1,0:T(8,128)(2,1)}), bf16[16,19,4096]{2,1,0:T(8,128)(2,1)}, u32[]{:S(2)}, u32[]{:S(2)}) %all-to-all-start.2) | async-done | bytes 2490400 | tf_op jit(solution)/shard_map/all_to_all | solution.py:58
  273.0 2.3 reshape.84
  275.4 0.0 all-gather.17.cloned.1.call-done
  275.4 1.4 copy-done.1
  276.8 2.6 fusion.4
  279.4 0.0 all-gather.15.cloned.1.call-done
  279.5 3.5 fusion.7
  283.0 2.7 fusion.11
  285.8 0.9 fusion.2
  286.7 0.5 copy-done.2
  287.2 2.3 fusion
  289.5 0.0 reduce-scatter.5.cloned.1.call-start
  289.6 2.2 convolution_convert_fusion
  291.9 39.0 %reduce-scatter.3.cloned.1.call-done = bf16[304,512]{1,0:T(8,128)(2,1)} async-done(((bf16[304,4096]{1,0:T(8,128)(2,1)}), bf16[304,512]{1,0:T(8,128)(2,1)}) %reduce-scatter.3.cloned.1.call-update) | async-done | bytes 311312 | tf_op jit(solution)/shard_map/reduce_scatter | solution.py:74
  330.9 1.8 convert_element_type.47
  332.7 7.5 %all-to-all-start.3 = ((bf16[16,19,512]{2,1,0:T(8,128)(2,1)}), bf16[16,19,512]{2,1,0:T(8,128)(2,1)S(1)}, u32[]{:S(2)}, u32[]{:S(2)}) async-start(bf16[16,19,512]{2,1,0:T(8,128)(2,1)} %convert_element_type.47), calls=%async_computation.4 | async-start | bytes 786432 | tf_op jit(solution)/shard_map/all_to_all | solution.py:77
  340.3 13.6 %all-to-all-done.3 = bf16[16,19,512]{2,1,0:T(8,128)(2,1)S(1)} async-done(((bf16[16,19,512]{2,1,0:T(8,128)(2,1)}), bf16[16,19,512]{2,1,0:T(8,128)(2,1)S(1)}, u32[]{:S(2)}, u32[]{:S(2)}) %all-to-all-start.3) | async-done | bytes 311328 | tf_op jit(solution)/shard_map/all_to_all | solution.py:77
  353.9 0.1 reshape.85
  354.0 0.1 pad_convert_fusion
  354.1 0.8 gather_fusion.2
  354.9 0.8 gather_fusion.3
  355.7 0.8 gather_fusion.4
  356.5 0.8 gather_fusion.5
  357.3 0.8 gather_fusion.6
  358.1 0.8 gather_fusion.7
  358.9 0.8 gather_fusion.8
  359.7 0.8 gather_fusion.9
  360.5 0.9 add_convert_fusion
  361.4 4.8 %reduce-scatter.5.cloned.1.call-done = bf16[192,1024]{1,0:T(8,128)(2,1)} async-done(((bf16[192,4096]{1,0:T(8,128)(2,1)}), bf16[192,1024]{1,0:T(8,128)(2,1)}) %reduce-scatter.5.cloned.1.call-update) | async-done | bytes 393232 | tf_op jit(solution)/shard_map/reduce_scatter | solution.py:71
  (25 shorter events, 0.2 us)
Async XLA Ops:
  8.0 48.9 %all-gather.9.cloned.1.call-start = ((), (), s32[]{:S(2)}) async-start(), calls=%async_computation.6 | async-start | bytes 1400832 | tf_op jit(solution)/shard_map/all_gather | solution.py:55
  8.7 90.7 %all-gather.11.cloned.1.call-start = ((), (), s32[]{:S(2)}) async-start(), calls=%async_computation.7 | async-start | bytes 1400832 | tf_op jit(solution)/shard_map/all_gather | solution.py:54
  24.7 92.5 %all-to-all-start = ((bf16[16,1,19]{2,1,0:T(2,128)(2,1)}), bf16[16,1,19]{2,1,0:T(2,128)(2,1)S(1)}, u32[]{:S(2)}, u32[]{:S(2)}) async-start(bf16[16,1,19]{2,1,0:T(2,128)(2,1)} %all_to_all.20), calls=%async_computation | async-start | bytes 16384 | tf_op jit(solution)/shard_map/all_to_all | solution.py:60
  117.3 79.2 %all-to-all-start.1 = ((bf16[16,19,4096]{2,1,0:T(8,128)(2,1)}), bf16[16,19,4096]{2,1,0:T(8,128)(2,1)S(1)}, u32[]{:S(2)}, u32[]{:S(2)}) async-start(bf16[16,19,4096]{2,1,0:T(8,128)(2,1)} %get-tuple-element.10), calls=%async_computation.1 | async-start | bytes 6291456 | tf_op jit(solution)/shard_map/all_to_all | solution.py:59
  124.7 150.7 %all-gather.17.cloned.1.call-start = ((), (), s32[]{:S(2)}) async-start(), calls=%async_computation.12 | async-start | bytes 1966080 | tf_op jit(solution)/shard_map/all_gather | solution.py:66
  196.5 76.5 %all-to-all-start.2 = ((bf16[16,19,4096]{2,1,0:T(8,128)(2,1)}), bf16[16,19,4096]{2,1,0:T(8,128)(2,1)}, u32[]{:S(2)}, u32[]{:S(2)}) async-start(bf16[16,19,4096]{2,1,0:T(8,128)(2,1)} %get-tuple-element.11), calls=%async_computation.2 | async-start | bytes 6291456 | tf_op jit(solution)/shard_map/all_to_all | solution.py:58
  201.2 78.3 %all-gather.15.cloned.1.call-start = ((), (), s32[]{:S(2)}) async-start(), calls=%async_computation.11 | async-start | bytes 1966080 | tf_op jit(solution)/shard_map/all_gather | solution.py:67
  201.8 81.2 %all-gather.13.cloned.1.call-start = ((), (), s32[]{:S(2)}) async-start(), calls=%async_computation.10 | async-start | bytes 1966080 | tf_op jit(solution)/shard_map/all_gather | solution.py:68
  202.4 128.5 %reduce-scatter.3.cloned.1.call-start = ((), (), s32[]{:S(2)}) async-start(), calls=%async_computation.8 | async-start | bytes 2801664 | tf_op jit(solution)/shard_map/reduce_scatter | solution.py:74
  275.4 1.5 copy-start.1
  279.4 3.6 copy-start
  283.0 2.7 copy-start.3
  285.8 1.4 copy-start.2
  289.5 76.7 %reduce-scatter.5.cloned.1.call-start = ((), (), s32[]{:S(2)}) async-start(), calls=%async_computation.9 | async-start | bytes 1966080 | tf_op jit(solution)/shard_map/reduce_scatter | solution.py:71
  332.7 21.2 %all-to-all-start.3 = ((bf16[16,19,512]{2,1,0:T(8,128)(2,1)}), bf16[16,19,512]{2,1,0:T(8,128)(2,1)S(1)}, u32[]{:S(2)}, u32[]{:S(2)}) async-start(bf16[16,19,512]{2,1,0:T(8,128)(2,1)} %convert_element_type.47), calls=%async_computation.4 | async-start | bytes 786432 | tf_op jit(solution)/shard_map/all_to_all | solution.py:77
Sparse Core Ops, SparseCore 0:
  10.9 45.9 all-gather.8
  59.0 40.4 all-gather.10
  289.7 41.1 reduce-scatter.2
  334.4 31.7 reduce-scatter.4
Sparse Core Ops, SparseCore 1:
  127.3 30.4 all-gather.16
  203.8 30.4 all-gather.14
  236.2 31.8 all-gather.12
where the time goes:
time: 374 us
  waiting for transfers between devices  234 us (63%)
  local copies, waits for them, and re-layouts  71.7 us (19%)
  starting transfers between devices  30.6 us (8%)
  between operations  15.8 us (4%)
  matrix products  14.3 us (4%)
  other arithmetic  6.76 us (2%)
    all_to_all x1, waiting for transfers between devices, local(): lax.all_to_all(pack(full_dy), 'expert', split_axis=0, concat_axis=0, tile...  71.2 us
    all_to_all x1, waiting for transfers between devices, local(): lax.all_to_all(pack(full_x), 'expert', split_axis=0, concat_axis=0, tiled...  68.2 us
    reduce_scatter x1, waiting for transfers between devices, local(): lax.psum_scatter(d_part_b.astype(jnp.float32).astype(jnp.bfloat16), 'etp'...  39 us
    all_gather x1, waiting for transfers between devices, local(): lax.all_gather(tokens, 'etp', axis=1, tiled=True)  30.9 us
    gather x4, local copies, waits for them, and re-layouts, pack(): source[owner]  24.5 us
    all_to_all x1, waiting for transfers between devices, local(): lax.all_to_all(summed.reshape(width, CAP, summed.shape[1]).astype(jnp.bfl...  13.6 us
    scatter x1, local copies, waits for them, and re-layouts, local(): jnp.zeros((slots + 1,), jnp.bfloat16).at[flat_all].set(gates.reshape(-1))  12.6 us
    scatter x1, local copies, waits for them, and re-layouts, local(): filled = jnp.zeros((slots + 1,), jnp.bool_).at[flat_all].set(True)[:slots]  11.4 us
  transfers between devices with their start and end apart: 11, of which 7 were waited for; matrix products, arithmetic and copies ran while one was open for 23% of the time, Pallas kernels for 0%

commit v1 on v0

--- a/solution.py
+++ b/solution.py
@@ -51,7 +51,9 @@
         return rows.reshape(width, CAP, source.shape[1])
 
     full_x, full_dy = (
-        lax.all_gather(tokens, "etp", axis=1, tiled=True),
+        jnp.concatenate(
+            lax.all_to_all(jnp.stack([tokens] * lax.axis_size("etp")), "etp", 0, 0), axis=1
+        ),
         lax.all_gather(cotangent, "etp", axis=1, tiled=True),
     )
     recv_x, recv_dy, recv_gate = (

time: 374 us -> 346 us (0.925)
  waiting for transfers between devices: 234 us -> 201 us
  starting transfers between devices: 30.6 us -> 40.5 us
  local copies, waits for them, and re-layouts: 71.7 us -> 67.6 us
    all_gather x1 -> x0, waiting for transfers between devices: 30.9 us -> none  [local(): lax.all_gather(tokens, 'etp', axis=1, tiled=True)]
    all_to_all x0 -> x1, starting transfers between devices: none -> 9.29 us  [local(): lax.all_to_all(jnp.stack([tokens] * lax.axis_size('etp')), 'etp', 0, 0)]
    gather x4, local copies, waits for them, and re-layouts: 24.5 us -> 18.8 us  [pack(): source[owner]]
  transfers between devices with their start and end apart: 11 -> 11, of which waited for: 7 -> 6; matrix products, arithmetic and copies ran while one was open for 23% -> 22% of each run, Pallas kernels for 0% -> 0%
where the time goes in v1:
time: 346 us; the launch traced here: 345 us
  waiting for transfers between devices  201 us (58%)
  local copies, waits for them, and re-layouts  67.6 us (20%)
  starting transfers between devices  40.5 us (12%)
  between operations  15.9 us (5%)
  matrix products  14.3 us (4%)
  other arithmetic  6.03 us (2%)
    all_to_all x1, waiting for transfers between devices, local(): lax.all_to_all(pack(full_dy), 'expert', split_axis=0, concat_axis=0, tile...  71.2 us
    all_to_all x1, waiting for transfers between devices, local(): lax.all_to_all(pack(full_x), 'expert', split_axis=0, concat_axis=0, tiled...  68.2 us
    reduce_scatter x1, waiting for transfers between devices, local(): lax.psum_scatter(d_part_b.astype(jnp.float32).astype(jnp.bfloat16), 'etp'...  40.7 us
    gather x4, local copies, waits for them, and re-layouts, pack(): source[owner]  18.8 us
    all_to_all x1, waiting for transfers between devices, local(): lax.all_to_all(summed.reshape(width, CAP, summed.shape[1]).astype(jnp.bfl...  13.6 us
    scatter x1, local copies, waits for them, and re-layouts, local(): jnp.zeros((slots + 1,), jnp.bfloat16).at[flat_all].set(gates.reshape(-1))  12.8 us
    all_to_all x1, starting transfers between devices, local(): lax.all_to_all(slot_gate, 'expert', split_axis=0, concat_axis=0, tiled=True)  11.5 us
    scatter x1, local copies, waits for them, and re-layouts, local(): filled = jnp.zeros((slots + 1,), jnp.bool_).at[flat_all].set(True)[:slots]  11.2 us
  transfers between devices with their start and end apart: 11, of which 6 were waited for; matrix products, arithmetic and copies ran while one was open for 22% of the time, Pallas kernels for 0%

profile of v1, /device:TPU:8, one launch (start us, length us, event | category | flops | bytes accessed | tf_op | source)
XLA Modules:
  0.0 345.5 jit_solution(9665939813137873433)
XLA Ops:
  8.0 2.1 stack.2
  10.1 9.3 %all-to-all-start.2 = ((bf16[8,152,512]{2,1,0:T(8,128)(2,1)}), bf16[8,152,512]{2,1,0:T(8,128)(2,1)S(1)}, u32[]{:S(2)}, u32[]{:S(2)}) async-start(bf16[8,152,512]{2,1,0:T(8,128)(2,1)} %stack.2), calls=%async_computation.2 | async-start | bytes 2490368 | tf_op jit(solution)/shard_map/all_to_all | solution.py:55
  19.4 0.7 all-gather.8.cloned.1.call-update
  20.1 0.1 copy.12
  20.2 0.1 reshape.88
  20.4 0.1 reshape.197
  20.5 11.2 %scatter_custom_fusion.1 = pred[305]{0:T(512)(128)(4,1)S(1)} fusion(s32[1216]{0:T(1024)S(1)} %fusion.18, pred[1216]{0:T(1024)(128)(4,1)S(1)} %broadcast.68, pred[]{:T(512)} %constant.14.clone.1), kind=kCustom, calls=%fused_computation.62 | custom fusion | bytes 306 | tf_op jit(solution)/shard_map/scatter | solution.py:45
  31.7 0.1 broadcast_in_dim.63
  31.8 0.1 copy.13
  32.0 0.1 reshape.181
  32.1 12.8 %scatter_custom_fusion = bf16[305]{0:T(512)(128)(2,1)S(1)} fusion(s32[1216]{0:T(1024)S(1)} %fusion.18, bf16[1216]{0:T(1024)(128)(2,1)S(1)} %reshape.181, bf16[]{:T(256)} %constant.9.clone.1), kind=kCustom, calls=%fused_computation.64 | custom fusion | bytes 612 | tf_op jit(solution)/shard_map/scatter | solution.py:46
  44.9 0.7 all_to_all.24
  45.6 6.4 %scatter_custom_fusion.2 = s32[305]{0:T(512)S(1)} fusion(s32[1216]{0:T(1024)S(1)} %fusion.18, s32[1216]{0:T(1024)S(1)} %reshape.197, s32[]{:T(128)} %constant.10.clone.1), kind=kCustom, calls=%fused_computation.60 | custom fusion | bytes 1224 | tf_op jit(solution)/shard_map/scatter | solution.py:44
  52.0 0.8 all-to-all-done.2
  52.8 11.5 %all-to-all-start = ((bf16[16,1,19]{2,1,0:T(2,128)(2,1)}), bf16[16,1,19]{2,1,0:T(2,128)(2,1)S(1)}, u32[]{:S(2)}, u32[]{:S(2)}) async-start(bf16[16,1,19]{2,1,0:T(2,128)(2,1)} %all_to_all.24), calls=%async_computation | async-start | bytes 16384 | tf_op jit(solution)/shard_map/all_to_all | solution.py:62
  64.3 0.1 copy.16
  64.5 3.8 %gather_fusion.1 = bf16[304,4096]{1,0:T(8,128)(2,1)} fusion(bf16[152,4096]{1,0:T(8,128)(2,1)S(1)} %bitcast.32, s32[1024]{0:T(1024)S(1)} %pad_clamp_fusion.8), kind=kCustom, calls=%fused_computation.1 | custom fusion | bytes 4981952 | tf_op jit(solution)/shard_map/gather | solution.py:50
  68.3 2.2 gather.37
  70.4 0.0 all-gather.8.cloned.1.call-done
  70.5 9.5 %gather_fusion = bf16[304,4096]{1,0:T(8,128)(2,1)} fusion(bf16[152,4096]{1,0:T(8,128)(2,1)} %all-gather.8.cloned.1.call-done, s32[1024]{0:T(1024)S(1)} %pad_clamp_fusion.8), kind=kCustom, calls=%fused_computation | custom fusion | bytes 4981952 | tf_op jit(solution)/shard_map/gather | solution.py:50
  79.9 3.4 gather.35
  83.3 5.0 %broadcast_select_fusion.1 = (bf16[16,19,4096]{2,1,0:T(8,128)(2,1)}, bf16[16,19,4096]{2,1,0:T(8,128)(2,1)}) fusion(bf16[16,19,4096]{2,1,0:T(8,128)(2,1)} %gather.35, pred[16,19]{1,0:T(8,128)(4,1)S(1)} %broadcast_in_dim.63, bf16[16,19,4096]{2,1,0:T(8,128)(2,1)S(1)} %gather.37), kind=kLoop, calls=%fused_computation.18 | loop fusion | flops 2490368 | bytes 9961776 | tf_op jit(solution)/shard_map/jit(_where)/select_n | solution.py:50
  88.3 7.3 %all-to-all-start.1 = ((bf16[16,19,4096]{2,1,0:T(8,128)(2,1)}), bf16[16,19,4096]{2,1,0:T(8,128)(2,1)S(1)}, u32[]{:S(2)}, u32[]{:S(2)}) async-start(bf16[16,19,4096]{2,1,0:T(8,128)(2,1)} %get-tuple-element.10), calls=%async_computation.1 | async-start | bytes 6291456 | tf_op jit(solution)/shard_map/all_to_all | solution.py:61
  95.6 0.0 all-gather.14.cloned.1.call-start
  95.7 0.5 all-gather.14.cloned.1.call-update
  96.2 71.2 %all-to-all-done.1 = bf16[16,19,4096]{2,1,0:T(8,128)(2,1)S(1)} async-done(((bf16[16,19,4096]{2,1,0:T(8,128)(2,1)}), bf16[16,19,4096]{2,1,0:T(8,128)(2,1)S(1)}, u32[]{:S(2)}, u32[]{:S(2)}) %all-to-all-start.1) | async-done | bytes 2490400 | tf_op jit(solution)/shard_map/all_to_all | solution.py:61
  167.4 4.7 %all-to-all-start.3 = ((bf16[16,19,4096]{2,1,0:T(8,128)(2,1)}), bf16[16,19,4096]{2,1,0:T(8,128)(2,1)}, u32[]{:S(2)}, u32[]{:S(2)}) async-start(bf16[16,19,4096]{2,1,0:T(8,128)(2,1)} %get-tuple-element.11), calls=%async_computation.3 | async-start | bytes 6291456 | tf_op jit(solution)/shard_map/all_to_all | solution.py:60
  172.1 0.0 all-gather.12.cloned.1.call-start
  172.1 0.5 all-gather.12.cloned.1.call-update
  172.7 0.0 all-gather.10.cloned.1.call-start
  172.7 0.5 all-gather.10.cloned.1.call-update
  173.3 0.3 reduce-scatter.3.cloned.1.call-start
  173.6 0.1 reshape.96
  173.7 2.1 reshape.91
  175.7 68.2 %all-to-all-done.3 = bf16[16,19,4096]{2,1,0:T(8,128)(2,1)} async-done(((bf16[16,19,4096]{2,1,0:T(8,128)(2,1)}), bf16[16,19,4096]{2,1,0:T(8,128)(2,1)}, u32[]{:S(2)}, u32[]{:S(2)}) %all-to-all-start.3) | async-done | bytes 2490400 | tf_op jit(solution)/shard_map/all_to_all | solution.py:60
  243.9 2.3 reshape.94
  246.3 0.0 all-gather.14.cloned.1.call-done
  246.3 1.4 copy-done.1
  247.7 2.6 fusion.4
  250.3 0.0 all-gather.12.cloned.1.call-done
  250.4 3.5 %fusion.7 = f32[304,192]{0,1:T(8,128)S(1)} fusion(bf16[304,4096]{1,0:T(8,128)(2,1)} %copy-done.1, bf16[1,4096,192]{1,2,0:T(8,128)(2,1)} %all-gather.12.cloned.1.call-done), kind=kOutput, calls=%fused_computation.25 | convolution fusion | flops 478150656 | bytes 4296704 | tf_op jit(solution)/shard_map/dot_general | solution.py:11
  253.9 0.0 all-gather.10.cloned.1.call-done
  253.9 2.7 fusion.11
  256.6 0.9 fusion.2
  257.6 0.5 copy-done.2
  258.0 2.4 fusion
  260.4 0.0 reduce-scatter.5.cloned.1.call-start
  260.5 2.3 convolution_convert_fusion
  262.8 40.7 %reduce-scatter.3.cloned.1.call-done = bf16[304,512]{1,0:T(8,128)(2,1)} async-done(((bf16[304,4096]{1,0:T(8,128)(2,1)}), bf16[304,512]{1,0:T(8,128)(2,1)}) %reduce-scatter.3.cloned.1.call-update) | async-done | bytes 311312 | tf_op jit(solution)/shard_map/reduce_scatter | solution.py:76
  303.5 1.8 convert_element_type.47
  305.3 7.3 %all-to-all-start.4 = ((bf16[16,19,512]{2,1,0:T(8,128)(2,1)}), bf16[16,19,512]{2,1,0:T(8,128)(2,1)S(1)}, u32[]{:S(2)}, u32[]{:S(2)}) async-start(bf16[16,19,512]{2,1,0:T(8,128)(2,1)} %convert_element_type.47), calls=%async_computation.5 | async-start | bytes 786432 | tf_op jit(solution)/shard_map/all_to_all | solution.py:79
  312.7 13.6 %all-to-all-done.4 = bf16[16,19,512]{2,1,0:T(8,128)(2,1)S(1)} async-done(((bf16[16,19,512]{2,1,0:T(8,128)(2,1)}), bf16[16,19,512]{2,1,0:T(8,128)(2,1)S(1)}, u32[]{:S(2)}, u32[]{:S(2)}) %all-to-all-start.4) | async-done | bytes 311328 | tf_op jit(solution)/shard_map/all_to_all | solution.py:79
  326.3 0.1 reshape.95
  326.4 0.1 pad_convert_fusion
  326.5 0.8 gather_fusion.2
  327.3 0.8 gather_fusion.3
  328.1 0.8 gather_fusion.4
  328.9 0.8 gather_fusion.5
  329.7 0.8 gather_fusion.6
  330.5 0.8 gather_fusion.7
  331.3 0.8 gather_fusion.8
  332.1 0.8 gather_fusion.9
  332.9 0.9 add_convert_fusion
  333.8 4.3 %reduce-scatter.5.cloned.1.call-done = bf16[192,1024]{1,0:T(8,128)(2,1)} async-done(((bf16[192,4096]{1,0:T(8,128)(2,1)}), bf16[192,1024]{1,0:T(8,128)(2,1)}) %reduce-scatter.5.cloned.1.call-update) | async-done | bytes 393232 | tf_op jit(solution)/shard_map/reduce_scatter | solution.py:73
  (32 shorter events, 0.2 us)
Async XLA Ops:
  8.0 12.1 %copy-start.5 = (s32[152,8]{0,1:T(8,128)S(1)}, s32[152,8]{0,1:T(8,128)}, u32[]{:S(2)}) copy-start(s32[152,8]{0,1:T(8,128)} %param.11) | copy-start | bytes 14596
  8.0 12.1 %copy-start.4 = (s32[152,8]{0,1:T(8,128)S(1)}, s32[152,8]{0,1:T(8,128)}, u32[]{:S(2)}) copy-start(s32[152,8]{0,1:T(8,128)} %param.12) | copy-start | bytes 14596
  8.0 23.8 %copy-start.6 = (bf16[152,8]{0,1:T(8,128)(2,1)S(1)}, bf16[152,8]{0,1:T(8,128)(2,1)}, u32[]{:S(2)}) copy-start(bf16[152,8]{0,1:T(8,128)(2,1)} %param.10) | copy-start | bytes 7300
  10.1 42.8 %all-to-all-start.2 = ((bf16[8,152,512]{2,1,0:T(8,128)(2,1)}), bf16[8,152,512]{2,1,0:T(8,128)(2,1)S(1)}, u32[]{:S(2)}, u32[]{:S(2)}) async-start(bf16[8,152,512]{2,1,0:T(8,128)(2,1)} %stack.2), calls=%async_computation.2 | async-start | bytes 2490368 | tf_op jit(solution)/shard_map/all_to_all | solution.py:55
  19.4 51.1 %all-gather.8.cloned.1.call-start = ((), (), s32[]{:S(2)}) async-start(), calls=%async_computation.7 | async-start | bytes 1400832 | tf_op jit(solution)/shard_map/all_gather | solution.py:57
  52.8 35.4 %all-to-all-start = ((bf16[16,1,19]{2,1,0:T(2,128)(2,1)}), bf16[16,1,19]{2,1,0:T(2,128)(2,1)S(1)}, u32[]{:S(2)}, u32[]{:S(2)}) async-start(bf16[16,1,19]{2,1,0:T(2,128)(2,1)} %all_to_all.24), calls=%async_computation | async-start | bytes 16384 | tf_op jit(solution)/shard_map/all_to_all | solution.py:62
  88.3 79.1 %all-to-all-start.1 = ((bf16[16,19,4096]{2,1,0:T(8,128)(2,1)}), bf16[16,19,4096]{2,1,0:T(8,128)(2,1)S(1)}, u32[]{:S(2)}, u32[]{:S(2)}) async-start(bf16[16,19,4096]{2,1,0:T(8,128)(2,1)} %get-tuple-element.10), calls=%async_computation.1 | async-start | bytes 6291456 | tf_op jit(solution)/shard_map/all_to_all | solution.py:61
  95.6 150.7 %all-gather.14.cloned.1.call-start = ((), (), s32[]{:S(2)}) async-start(), calls=%async_computation.12 | async-start | bytes 1966080 | tf_op jit(solution)/shard_map/all_gather | solution.py:68
  167.4 76.5 %all-to-all-start.3 = ((bf16[16,19,4096]{2,1,0:T(8,128)(2,1)}), bf16[16,19,4096]{2,1,0:T(8,128)(2,1)}, u32[]{:S(2)}, u32[]{:S(2)}) async-start(bf16[16,19,4096]{2,1,0:T(8,128)(2,1)} %get-tuple-element.11), calls=%async_computation.3 | async-start | bytes 6291456 | tf_op jit(solution)/shard_map/all_to_all | solution.py:60
  172.1 78.3 %all-gather.12.cloned.1.call-start = ((), (), s32[]{:S(2)}) async-start(), calls=%async_computation.11 | async-start | bytes 1966080 | tf_op jit(solution)/shard_map/all_gather | solution.py:69
  172.7 81.2 %all-gather.10.cloned.1.call-start = ((), (), s32[]{:S(2)}) async-start(), calls=%async_computation.10 | async-start | bytes 1966080 | tf_op jit(solution)/shard_map/all_gather | solution.py:70
  173.3 130.2 %reduce-scatter.3.cloned.1.call-start = ((), (), s32[]{:S(2)}) async-start(), calls=%async_computation.8 | async-start | bytes 2801664 | tf_op jit(solution)/shard_map/reduce_scatter | solution.py:76
  246.2 1.5 copy-start.1
  250.3 3.6 %copy-start = (bf16[304,4096]{1,0:T(8,128)(2,1)S(1)}, bf16[304,4096]{1,0:T(8,128)(2,1)}, u32[]{:S(2)}) copy-start(bf16[304,4096]{1,0:T(8,128)(2,1)} %reshape.91) | copy-start | bytes 7471108
  253.9 2.7 copy-start.3
  256.6 1.4 copy-start.2
  260.4 77.7 %reduce-scatter.5.cloned.1.call-start = ((), (), s32[]{:S(2)}) async-start(), calls=%async_computation.9 | async-start | bytes 1966080 | tf_op jit(solution)/shard_map/reduce_scatter | solution.py:73
  305.3 21.0 %all-to-all-start.4 = ((bf16[16,19,512]{2,1,0:T(8,128)(2,1)}), bf16[16,19,512]{2,1,0:T(8,128)(2,1)S(1)}, u32[]{:S(2)}, u32[]{:S(2)}) async-start(bf16[16,19,512]{2,1,0:T(8,128)(2,1)} %convert_element_type.47), calls=%async_computation.5 | async-start | bytes 786432 | tf_op jit(solution)/shard_map/all_to_all | solution.py:79
Sparse Core Ops, SparseCore 0:
  22.3 45.9 all-gather.7
  260.5 42.8 reduce-scatter.2
  307.2 30.9 reduce-scatter.4
Sparse Core Ops, SparseCore 1:
  98.2 31.4 all-gather.13
  174.7 31.3 all-gather.11
  208.0 31.8 all-gather.9
